TPU v7x, 32 devices: a whole 2x2x4 slice. The times are simulated.
32 devices in a mesh: run: 1, row: 16 (over z, y, core), col: 1, seg: 2 (over x).
Axes of the slice: x: 2, y: 2, z: 4, core: 2. Of those that a mesh axis runs over, the one named last changes fastest.
Arguments:
- traces: bfloat16 [2, 1024, 2048], P(('run', 'seg'), 'row', 'col'), may hold values from -30 to 30
- live_mask: int32 [1024], P(('run', 'row')), may hold values 0 or 1
- sources: int32 [64], replicated, may hold values from 0 to 1023
- owners: int32 [64, 1], replicated, may hold values from 0 to 15; in each aligned block of 64 rows (0 to 63, 64 to 127, ...) at most 12 rows name the same one
Outputs:
- gathers: bfloat16 [192, 16, 64, 256], P(('run', 'row'), None, ('col', 'seg'))
Inputs may be any that keep to these rules, and one draw needn't show every extreme that they name: `owners`: at most 12 sources share an owner, and some owner has exactly 12.
All inputs are finite; a program needn't handle non-finite values. No bound on the sum of `live_mask` on one device may be relied on, other than what follows from the above.
Results may differ from a plain program's by a relative error of at most 0.024.
Values may be sent and summed in bfloat16 or wider, within the bound.
No kernel may reach another device: no remote copies, remote signals or barrier semaphores. Data moves between devices by JAX's collectives and lax.ppermute only.
A program may use at most 64 MiB of HBM per device.

v0:
```python
import math
import jax
import jax.numpy as jnp
from jax import lax
from jax.sharding import PartitionSpec as P

NT = 2048
NF = 1024
LAGS = 256
BAND = 64
two_pi = 2.0 * math.pi


def turn_table(first_ids, second_ids, period):
    product = first_ids[:, None] * second_ids[None, :] % period
    return product.astype(jnp.float32) * (two_pi / period)


def lag_matrix(bin_ids):
    lag_ids = jnp.arange(LAGS, dtype=jnp.int32) - LAGS // 2 + NT
    lag_angles = turn_table(bin_ids, lag_ids, NT)
    return jnp.concatenate(
        [jnp.cos(lag_angles).astype(jnp.bfloat16), -jnp.sin(lag_angles).astype(jnp.bfloat16)],
        axis=0,
    )


def correlate(recv_real, recv_imag, real_source, imag_source, lag_table):
    cross_real = (
        real_source[:, None, :] * recv_real[:, :, None]
        + imag_source[:, None, :] * recv_imag[:, :, None]
    ).astype(jnp.bfloat16)
    cross_imag = (
        imag_source[:, None, :] * recv_real[:, :, None]
        - real_source[:, None, :] * recv_imag[:, :, None]
    ).astype(jnp.bfloat16)
    stacked_cross = jnp.concatenate([cross_real, cross_imag], axis=0)
    return jnp.einsum("fl,fgv->gvl", lag_table, stacked_cross, preferred_element_type=jnp.float32)


def local(traces, live_mask, sources, owners):
    col_count = lax.axis_size("col")
    seg_count = lax.axis_size("seg")
    row_count = lax.axis_size("row")
    samples = traces[0]
    channels = samples.shape[0]
    local_width = samples.shape[1]
    num_sources = sources.shape[0]
    first_sample = lax.axis_index("col") * local_width
    half_bins = NF // col_count
    sample_ids = first_sample + jnp.arange(local_width, dtype=jnp.int32)
    bin_ids = jnp.arange(half_bins * lax.axis_size("col"), dtype=jnp.int32)
    angles = turn_table(sample_ids, bin_ids, NT)
    cosine = jnp.cos(angles).astype(jnp.bfloat16)
    sine_table = jnp.sin(angles).astype(jnp.bfloat16)
    real_part = jnp.einsum("tf,ct->fc", cosine, samples, preferred_element_type=jnp.float32)
    imag_part = -jnp.einsum("tf,ct->fc", sine_table, samples, preferred_element_type=jnp.float32)
    spectra = lax.psum_scatter(
        jnp.concatenate([real_part, imag_part], axis=1).astype(jnp.bfloat16),
        "col",
        scatter_dimension=0,
        tiled=True,
    ).astype(jnp.float32)
    squares = (spectra * spectra).reshape(half_bins // BAND, BAND, 2, channels)
    band_power = jnp.sum(squares, axis=(1, 2)) / (2 * BAND) + 1e-05
    scaling = live_mask.astype(jnp.float32)[None, :] / jnp.sqrt(band_power)
    scaling = jnp.repeat(scaling, BAND, axis=0)
    whitened = (
        (spectra.reshape(half_bins, 2, channels) * scaling[:, None, :])
        .reshape(half_bins, 2 * channels)
        .astype(jnp.bfloat16)
    )
    white_real = whitened[:, :channels]
    white_imag = whitened[:, channels:]
    everyone = lax.all_gather(whitened, "row", axis=1, tiled=True)
    block_ids = sources // channels
    within = sources % channels
    real_cols = block_ids * (2 * channels) + within
    source_real = jnp.take(everyone, real_cols, axis=1)
    source_imag = jnp.take(everyone, real_cols + channels, axis=1)
    receivers = channels // (col_count * seg_count)
    bin_ids = lax.axis_index("col") * half_bins + jnp.arange(half_bins, dtype=jnp.int32)
    lag_table = lag_matrix(bin_ids)
    real_source = source_real.astype(jnp.float32)
    imag_source = source_imag.astype(jnp.float32)

    def one_group(offset):
        recv_real = lax.dynamic_slice_in_dim(white_real, offset, receivers, 1).astype(jnp.float32)
        recv_imag = lax.dynamic_slice_in_dim(white_imag, offset, receivers, 1).astype(jnp.float32)
        return correlate(recv_real, recv_imag, real_source, imag_source, lag_table)

    offsets = (
        jnp.arange(receivers * lax.axis_size(("col", "seg")) // receivers, dtype=jnp.int32)
        * receivers
    )
    blocks = lax.map(one_group, offsets)
    stacked = lax.psum_scatter(
        blocks.reshape(receivers * lax.axis_size(("col", "seg")), num_sources, LAGS).astype(
            jnp.bfloat16
        ),
        ("col", "seg"),
        scatter_dimension=0,
        tiled=True,
    ).astype(jnp.float32)
    mean_sq = jnp.mean(stacked * stacked, axis=-1, keepdims=True)
    normed = (stacked / jnp.sqrt(mean_sq + 1e-06)).astype(jnp.bfloat16)
    capacity = 3 * num_sources // row_count
    owner_ids = owners[:, 0]
    order_ids = jnp.arange(num_sources, dtype=jnp.int32)
    earlier = (owner_ids[:, None] == owner_ids[None, :]) & (order_ids[None, :] < order_ids[:, None])
    slot_rank = jnp.sum(earlier.astype(jnp.int32), axis=1)
    slot_ids = owner_ids * capacity + slot_rank
    placing = (
        jnp.arange(row_count * capacity, dtype=jnp.int32)[:, None] == slot_ids[None, :]
    ).astype(jnp.bfloat16)
    outgoing = jnp.einsum(
        "sv,gvl->sgl", placing, normed, preferred_element_type=jnp.float32
    ).astype(jnp.bfloat16)
    return lax.all_to_all(outgoing[:, None], "row", split_axis=0, concat_axis=1, tiled=True)


def solution(mesh):
    placed = (P(("run", "seg"), "row", "col"), P(("run", "row")), P(), P())
    return jax.shard_map(
        local,
        mesh=mesh,
        in_specs=placed,
        out_specs=P(("run", "row"), None, ("col", "seg"), None),
        check_vma=False,
    )
```

profile of v0, /device:TPU:1, one launch (start us, length us, event | category | flops | bytes accessed | tf_op | source)
XLA Modules:
  0.0 271.0 jit_solution(1408020758581116476)
XLA Ops:
  6.5 0.0 copy-start
  6.5 0.0 all-gather.2.cloned.1.call-start
  6.5 0.9 copy-done
  7.5 31.3 %fusion.21 = bf16[1024,64]{0,1:T(8,128)(2,1)S(1)} fusion(bf16[1,64,2048]{2,1,0:T(8,128)(2,1)S(1)} %copy-done), kind=kOutput, calls=%fused_computation.35 | convolution fusion | flops 300023808 | bytes 393216 | tf_op jit(solution)/shard_map/tf,ct->fc/dot_general | solution.py:57
  38.8 0.0 copy-start.4
  38.8 31.2 %fusion.22 = bf16[1024,64]{0,1:T(8,128)(2,1)S(1)} fusion(bf16[1,64,2048]{2,1,0:T(8,128)(2,1)S(1)} %copy-done), kind=kOutput, calls=%fused_computation.36 | convolution fusion | flops 299958272 | bytes 393216 | tf_op jit(solution)/shard_map/tf,ct->fc/dot_general | solution.py:56
  70.1 0.0 copy-start.3
  70.1 0.3 mul.149
  70.4 0.2 reduce_sum.28
  70.6 0.1 copy.15
  70.7 0.0 copy-done.4
  70.7 0.1 copy.16
  70.8 0.2 broadcast_in_dim.19
  71.0 0.2 mul.150
  71.2 0.8 multiply_convert_fusion
  72.0 0.0 all-gather.2.cloned.1.call-update
  72.0 0.0 reduce-scatter.2.cloned.1.call-start
  72.1 0.0 copy-done.3
  72.1 1.0 fusion.48
  73.1 4.2 %cosine_convert_fusion.4 = bf16[1024,256]{1,0:T(8,128)(2,1)S(1)} fusion(s32[256]{0:T(256)S(1)} %iota_add_fusion), kind=kLoop, calls=%fused_computation.43 | loop fusion | flops 3932160 | bytes 525312 | tf_op jit(solution)/shard_map/convert_element_type | solution.py:23
  77.3 4.0 %fusion.31 = bf16[1024,256]{1,0:T(8,128)(2,1)S(1)} fusion(s32[256]{0:T(256)S(1)} %iota_add_fusion), kind=kLoop, calls=%fused_computation.47 | loop fusion | flops 4718592 | bytes 525312 | tf_op jit(solution)/shard_map/neg | solution.py:23
  81.4 1.0 pad_maximum_fusion
  82.4 42.7 %all-gather.2.cloned.1.call-done = bf16[1024,2048]{0,1:T(8,128)(2,1)} async-done(((bf16[1024,128]{0,1:T(8,128)(2,1)}), bf16[1024,2048]{0,1:T(8,128)(2,1)}) %all-gather.2.cloned.1.call-update) | async-done | bytes 4194320 | tf_op jit(solution)/shard_map/all_gather | solution.py:75
  125.1 3.5 %gather_fusion = bf16[64,1024]{1,0:T(8,128)(2,1)S(1)} fusion(bf16[1024,2048]{0,1:T(8,128)(2,1)} %all-gather.2.cloned.1.call-done, s32[1024]{0:T(1024)S(1)} %pad_clamp_fusion.1), kind=kCustom, calls=%fused_computation.clone | custom fusion | bytes 262400 | tf_op jit(solution)/shard_map/jit(_take)/gather | solution.py:79
  128.6 3.5 %gather_fusion.1 = bf16[64,1024]{1,0:T(8,128)(2,1)S(1)} fusion(bf16[1024,2048]{0,1:T(8,128)(2,1)} %all-gather.2.cloned.1.call-done, s32[1024]{0:T(1024)S(1)} %pad_clamp_fusion), kind=kCustom, calls=%fused_computation.1.clone | custom fusion | bytes 262400 | tf_op jit(solution)/shard_map/jit(_take)/gather | solution.py:80
  132.2 0.1 bitcast_convert_fusion
  132.3 0.0 copy-start.5
  132.3 16.3 %while.10 = (s32[]{:T(128)}, bf16[2,32,64,256]{3,2,1,0:T(8,128)(2,1)S(1)}, f32[1024,64]{0,1:T(8,128)S(1)}, s32[2]{0:T(128)S(1)}, bf16[1024,64]{0,1:T(8,128)(2,1)...) while((s32[]{:T(128)}, ...), condition=%wide.region_3.5_spmd, body=%wide.region_2.4_spmd.sunk | while | flops 2181103616 | bytes 25297088 | solution.py:96
  132.3 0.7 dynamic_slice.15
  135.1 0.0 copy-start.2
  135.1 2.8 %add_convert_fusion.2 = (bf16[1024,32,64]{0,2,1:T(8,128)(2,1)S(1)}, bf16[1024,32,64]{0,2,1:T(8,128)(2,1)S(1)}) fusion(f32[1024,32]{0,1:T(8,128)S(1)} %get-tuple-element.129, f32[1024,64]{0,1:T(8,128)S(1)} %get-tuple-element.160, f32[1024,32]{0,1:T(8,128)S(1)} %get-tuple-element.130, f32[1024,64]{0,1:T(8,128)S(1)} %get-tuple-element.157), kind=kLoop, calls=%fused_computation.7.clone.1 | loop fusion | flops 16777216 | bytes 9175040 | tf_op jit(solution)/shard_map/while/body/eval_jaxpr/convert_element_type | solution.py:32
  137.9 0.0 copy-done.2
  137.9 2.5 bitcast_dynamic-update-slice_fusion.2
  140.5 0.7 dynamic_slice.15
  143.3 0.0 copy-start.2
  143.3 2.8 %add_convert_fusion.2 = (bf16[1024,32,64]{0,2,1:T(8,128)(2,1)S(1)}, bf16[1024,32,64]{0,2,1:T(8,128)(2,1)S(1)}) fusion(f32[1024,32]{0,1:T(8,128)S(1)} %get-tuple-element.129, f32[1024,64]{0,1:T(8,128)S(1)} %get-tuple-element.160, f32[1024,32]{0,1:T(8,128)S(1)} %get-tuple-element.130, f32[1024,64]{0,1:T(8,128)S(1)} %get-tuple-element.157), kind=kLoop, calls=%fused_computation.7.clone.1 | loop fusion | flops 16777216 | bytes 9175040 | tf_op jit(solution)/shard_map/while/body/eval_jaxpr/convert_element_type | solution.py:32
  146.1 0.0 copy-done.2
  146.1 2.5 bitcast_dynamic-update-slice_fusion.2
  148.7 0.0 copy-start.1
  148.7 1.3 copy-done.1
  150.0 0.0 reduce-scatter.2.cloned.1.call-update
  150.0 0.2 convert_reduce_fusion
  150.2 29.8 %reduce-scatter.2.cloned.1.call-done = bf16[32,64,256]{2,1,0:T(8,128)(2,1)} async-done(((bf16[64,64,256]{2,1,0:T(8,128)(2,1)}), bf16[32,64,256]{2,1,0:T(8,128)(2,1)}) %reduce-scatter.2.cloned.1.call-update) | async-done | bytes 1048592 | tf_op jit(solution)/shard_map/reduce_scatter | solution.py:97
  180.0 1.6 fusion.18
  181.6 2.3 convert_bitcast_fusion
  184.0 1.8 copy.17
  185.7 76.3 %all_to_all.18 = bf16[192,1,32,256]{3,2,1,0:T(8,128)(2,1)S(1)} all-to-all(bf16[192,1,32,256]{3,2,1,0:T(8,128)(2,1)S(1)} %copy.17), channel_id=1, replica_groups=mesh['run'=1,'row'=16,'col'=1,'seg'=2] {'row'}, dimensions={0} | all-to-all | bytes 6291456 | tf_op jit(solution)/shard_map/all_to_all | solution.py:119
  262.1 2.1 copy.18
  (16 shorter events, 0.2 us)
Async XLA Ops:
  6.5 1.0 copy-start
  6.5 118.6 %all-gather.2.cloned.1.call-start = ((), (), s32[]{:S(2)}) async-start(), calls=%async_computation.2 | async-start | bytes 4456448 | tf_op jit(solution)/shard_map/all_gather | solution.py:75
  38.8 31.9 %copy-start.4 = (s32[64]{0:T(128)S(1)}, s32[64]{0:T(128)}, u32[]{:S(2)}) copy-start(s32[64]{0:T(128)} %param.9) | copy-start | bytes 772
  70.1 2.0 copy-start.3
  72.0 108.0 %reduce-scatter.2.cloned.1.call-start = ((), (), s32[]{:S(2)}) async-start(), calls=%async_computation.3 | async-start | bytes 3145728 | tf_op jit(solution)/shard_map/reduce_scatter | solution.py:97
  132.3 17.7 %copy-start.5 = (s32[64,1]{0,1:T(1,128)S(1)}, s32[64,1]{0,1:T(1,128)}, u32[]{:S(2)}) copy-start(s32[64,1]{0,1:T(1,128)} %param.11) | copy-start | bytes 772
  135.1 2.8 %copy-start.2 = (bf16[2048,256]{1,0:T(8,128)(2,1)S(1)}, bf16[2048,256]{1,0:T(8,128)(2,1)}, u32[]{:S(2)}) copy-start(bf16[2048,256]{1,0:T(8,128)(2,1)} %get-tuple-element.162) | copy-start | bytes 3145732 | tf_op jit(solution)/shard_map/while
  143.3 2.8 %copy-start.2 = (bf16[2048,256]{1,0:T(8,128)(2,1)S(1)}, bf16[2048,256]{1,0:T(8,128)(2,1)}, u32[]{:S(2)}) copy-start(bf16[2048,256]{1,0:T(8,128)(2,1)} %get-tuple-element.162) | copy-start | bytes 3145732 | tf_op jit(solution)/shard_map/while
  148.7 1.3 copy-start.1
Sparse Core Ops, SparseCore 0:
  72.1 52.9 all-gather.1
  150.1 29.8 reduce-scatter.1
where the time goes:
time: 271 us
  blocking collectives  76.3 us (28%)
  waiting for transfers between devices  72.6 us (27%)
  matrix products  70 us (26%)
  other arithmetic  17.9 us (7%)
  local copies, waits for them, and re-layouts  16.3 us (6%)
  between operations  13.6 us (5%)
  loops' own time  4.26 us (2%)
    all_to_all x1, blocking collectives, local(): lax.all_to_all(outgoing[:, None], 'row', split_axis=0, concat_axis=1, til...  76.3 us
    all_gather x1, waiting for transfers between devices, local(): everyone = lax.all_gather(whitened, 'row', axis=1, tiled=True)  42.7 us
    dot_general x1, matrix products, local(): jnp.einsum('tf,ct->fc', sine_table, samples, preferred_element_type=jnp.f...  31.3 us
    dot_general x1, matrix products, local(): jnp.einsum('tf,ct->fc', cosine, samples, preferred_element_type=jnp.float32)  31.2 us
    reduce_scatter x1, waiting for transfers between devices, local(): lax.psum_scatter(blocks.reshape(receivers * lax.axis_size(('col', 'seg'))...  29.8 us
    convert_element_type x2, other arithmetic, correlate(): cross_real = (real_source[:, None, :] * recv_real[:, :, None] + imag_sour...  5.58 us
  transfers between devices with their start and end apart: 2, of which 2 were waited for; matrix products, arithmetic and copies ran while one was open for 4% of the time, Pallas kernels for 0%

commit v1 on v0

--- a/solution.py
+++ b/solution.py
@@ -72,7 +72,26 @@
     )
     white_real = whitened[:, :channels]
     white_imag = whitened[:, channels:]
-    everyone = lax.all_gather(whitened, "row", axis=1, tiled=True)
+    count, position, span = (lax.axis_size("row"), lax.axis_index("row"), whitened.shape[1])
+    upward = [(i, (i + 1) % count) for i in range(count)]
+    downward = [(i, (i - 1) % count) for i in range(count)]
+    result = jnp.zeros(
+        (*whitened.shape[:1], count * span, *whitened.shape[1 + 1 :]), whitened.dtype
+    )
+    result = lax.dynamic_update_slice_in_dim(result, whitened, position * span, axis=1)
+    from_left = from_right = whitened
+    halfway = count // 2
+    for lap in range(1, halfway + 1):
+        from_left = lax.ppermute(from_left, "row", upward)
+        result = lax.dynamic_update_slice_in_dim(
+            result, from_left, (position - lap) % count * span, axis=1
+        )
+        if lap < count - halfway:
+            from_right = lax.ppermute(from_right, "row", downward)
+            result = lax.dynamic_update_slice_in_dim(
+                result, from_right, (position + lap) % count * span, axis=1
+            )
+    everyone = result
     block_ids = sources // channels
     within = sources % channels
     real_cols = block_ids * (2 * channels) + within

time: 271 us -> 293 us (1.081)
  starting transfers between devices: 0.04 us -> 30.4 us
  waiting for transfers between devices: 72.6 us -> 47.5 us
  local copies, waits for them, and re-layouts: 16.3 us -> 33.2 us
    all_gather x1 -> x0, waiting for transfers between devices: 42.7 us -> none  [local(): everyone = lax.all_gather(whitened, 'row', axis=1, tiled=True)]
    ppermute x0 -> x15, starting transfers between devices: none -> 30.4 us  [the longest x7 23.1 us: local(): from_right = lax.ppermute(from_right, 'row', downward)]
    dynamic_update_slice x0 -> x16, local copies, waits for them, and re-layouts: none -> 15.4 us  [the longest x8 7.69 us: local(): lax.dynamic_update_slice_in_dim(result, from_left, (position - lap) % cou...]
    ppermute x0 -> x15, waiting for transfers between devices: none -> 11.3 us  [the longest x7 6.02 us: local(): from_right = lax.ppermute(from_right, 'row', downward)]
    reduce_scatter x1, waiting for transfers between devices: 29.8 us -> 36.1 us  [local(): lax.psum_scatter(blocks.reshape(receivers * lax.axis_size(('col', 'seg'))...]
  transfers between devices with their start and end apart: 2 -> 16, of which waited for: 2 -> 5; matrix products, arithmetic and copies ran while one was open for 4% -> 9% of each run, Pallas kernels for 0% -> 0%
where the time goes in v1:
time: 293 us; the launch traced here: 292 us
  blocking collectives  76.3 us (26%)
  matrix products  70 us (24%)
  waiting for transfers between devices  47.5 us (16%)
  local copies, waits for them, and re-layouts  33.2 us (11%)
  starting transfers between devices  30.4 us (10%)
  other arithmetic  16.9 us (6%)
  between operations  14 us (5%)
  loops' own time  4.24 us (1%)
    all_to_all x1, blocking collectives, local(): lax.all_to_all(outgoing[:, None], 'row', split_axis=0, concat_axis=1, til...  76.3 us
    reduce_scatter x1, waiting for transfers between devices, local(): lax.psum_scatter(blocks.reshape(receivers * lax.axis_size(('col', 'seg'))...  36.1 us
    dot_general x1, matrix products, local(): jnp.einsum('tf,ct->fc', sine_table, samples, preferred_element_type=jnp.f...  31.3 us
    dot_general x1, matrix products, local(): jnp.einsum('tf,ct->fc', cosine, samples, preferred_element_type=jnp.float32)  31.2 us
    ppermute x7, starting transfers between devices, local(): from_right = lax.ppermute(from_right, 'row', downward)  23.1 us
    dynamic_update_slice x8, local copies, waits for them, and re-layouts, local(): lax.dynamic_update_slice_in_dim(result, from_left, (position - lap) % cou...  7.69 us
    ppermute x8, starting transfers between devices, local(): from_left = lax.ppermute(from_left, 'row', upward)  7.32 us
    dynamic_update_slice x7, local copies, waits for them, and re-layouts, local(): lax.dynamic_update_slice_in_dim(result, from_right, (position + lap) % co...  6.95 us
  transfers between devices with their start and end apart: 16, of which 5 were waited for; matrix products, arithmetic and copies ran while one was open for 9% of the time, Pallas kernels for 0%

profile of v1, /device:TPU:1, one launch (start us, length us, event | category | flops | bytes accessed | tf_op | source)
XLA Modules:
  0.0 292.5 jit_solution(1718262741906529372)
XLA Ops:
  6.5 0.9 copy-done
  7.5 31.3 %fusion.21 = bf16[1024,64]{0,1:T(8,128)(2,1)S(1)} fusion(bf16[1,64,2048]{2,1,0:T(8,128)(2,1)S(1)} %copy-done), kind=kOutput, calls=%fused_computation.35 | convolution fusion | flops 300023808 | bytes 393216 | tf_op jit(solution)/shard_map/tf,ct->fc/dot_general | solution.py:57
  38.8 31.2 %fusion.22 = bf16[1024,64]{0,1:T(8,128)(2,1)S(1)} fusion(bf16[1,64,2048]{2,1,0:T(8,128)(2,1)S(1)} %copy-done), kind=kOutput, calls=%fused_computation.36 | convolution fusion | flops 299958272 | bytes 393216 | tf_op jit(solution)/shard_map/tf,ct->fc/dot_general | solution.py:56
  71.2 2.7 collective-permute-start
  73.9 3.9 %cosine_convert_fusion.4 = bf16[1024,256]{1,0:T(8,128)(2,1)S(1)} fusion(s32[256]{0:T(256)S(1)} %iota_add_fusion), kind=kLoop, calls=%fused_computation.43 | loop fusion | flops 3932160 | bytes 525312 | tf_op jit(solution)/shard_map/convert_element_type | solution.py:23
  77.9 4.0 %fusion.31 = bf16[1024,256]{1,0:T(8,128)(2,1)S(1)} fusion(s32[256]{0:T(256)S(1)} %iota_add_fusion), kind=kLoop, calls=%fused_computation.47 | loop fusion | flops 4718592 | bytes 525312 | tf_op jit(solution)/shard_map/neg | solution.py:23
  81.9 1.0 pad_maximum_fusion
  83.0 1.8 collective-permute-start.2
  84.8 1.3 collective-permute-start.3
  86.1 2.0 collective-permute-done.2
  88.1 2.5 collective-permute-start.4
  90.6 2.5 broadcast_in_dim.21
  93.1 0.7 constant_dynamic-update-slice_fusion.15
  93.8 3.9 %collective-permute-start.5 = (bf16[1024,128]{0,1:T(8,128)(2,1)}, bf16[1024,128]{0,1:T(8,128)(2,1)}, u32[]{:S(2)}, u32[]{:S(2)}) collective-permute-start(bf16[1024,128]{0,1:T(8,128)(2,1)} %collective-permute-done.3), channel_id=1, source_target_pairs={{0,30},{2,0},{4,2},{6,4},{8,6},{10,8},{12,10},{14,12},{16,14},{18,... | collective-permute-start | bytes 786440 | tf_op jit(solution)/shard_map/ppermute | solution.py:90
  98.2 0.7 constant_dynamic-update-slice_fusion.14
  98.9 3.9 %collective-permute-done.5 = bf16[1024,128]{0,1:T(8,128)(2,1)} collective-permute-done((bf16[1024,128]{0,1:T(8,128)(2,1)}, bf16[1024,128]{0,1:T(8,128)(2,1)}, u32[]{:S(2)}, u32[]{:S(2)}) %collective-permute-start.5) | collective-permute-done | bytes 262176 | tf_op jit(solution)/shard_map/ppermute | solution.py:90
  102.7 3.6 %collective-permute-start.7 = (bf16[1024,128]{0,1:T(8,128)(2,1)}, bf16[1024,128]{0,1:T(8,128)(2,1)S(1)}, u32[]{:S(2)}, u32[]{:S(2)}) collective-permute-start(bf16[1024,128]{0,1:T(8,128)(2,1)} %collective-permute-done.5), channel_id=1, source_target_pairs={{0,30},{2,0},{4,2},{6,4},{8,6},{10,8},{12,10},{14,12},{16,14},{18,... | collective-permute-start | bytes 786440 | tf_op jit(solution)/shard_map/ppermute | solution.py:90
  106.4 0.7 constant_dynamic-update-slice_fusion.13
  107.8 1.7 constant_dynamic-update-slice_fusion.11
  109.5 2.2 collective-permute-done.7
  111.6 3.6 %collective-permute-start.9 = (bf16[1024,128]{0,1:T(8,128)(2,1)S(1)}, bf16[1024,128]{0,1:T(8,128)(2,1)S(1)}, u32[]{:S(2)}, u32[]{:S(2)}) collective-permute-start(bf16[1024,128]{0,1:T(8,128)(2,1)S(1)} %collective-permute-done.7), channel_id=1, source_target_pairs={{0,30},{2,0},{4,2},{6,4},{8,6},{10,8},{12,10},{14,12},{16,14},{18,... | collective-permute-start | bytes 786440 | tf_op jit(solution)/shard_map/ppermute | solution.py:90
  115.2 1.7 constant_dynamic-update-slice_fusion.10
  116.8 1.7 constant_dynamic-update-slice_fusion.9
  118.5 1.7 constant_dynamic-update-slice_fusion.8
  120.2 4.6 %collective-permute-start.11 = (bf16[1024,128]{0,1:T(8,128)(2,1)S(1)}, bf16[1024,128]{0,1:T(8,128)(2,1)S(1)}, u32[]{:S(2)}, u32[]{:S(2)}) collective-permute-start(bf16[1024,128]{0,1:T(8,128)(2,1)S(1)} %collective-permute-done.9), channel_id=1, source_target_pairs={{0,30},{2,0},{4,2},{6,4},{8,6},{10,8},{12,10},{14,12},{16,14},{18,... | collective-permute-start | bytes 786440 | tf_op jit(solution)/shard_map/ppermute | solution.py:90
  124.8 0.7 constant_dynamic-update-slice_fusion.7
  125.5 0.7 constant_dynamic-update-slice_fusion.6
  127.0 6.1 %collective-permute-start.13 = (bf16[1024,128]{0,1:T(8,128)(2,1)S(1)}, bf16[1024,128]{0,1:T(8,128)(2,1)S(1)}, u32[]{:S(2)}, u32[]{:S(2)}) collective-permute-start(bf16[1024,128]{0,1:T(8,128)(2,1)S(1)} %collective-permute-done.11), channel_id=1, source_target_pairs={{0,30},{2,0},{4,2},{6,4},{8,6},{10,8},{12,10},{14,12},{16,14},{18,... | collective-permute-start | bytes 786440 | tf_op jit(solution)/shard_map/ppermute | solution.py:90
  133.1 0.7 constant_dynamic-update-slice_fusion.4
  134.1 0.7 constant_dynamic-update-slice_fusion.3
  134.9 0.7 constant_dynamic-update-slice_fusion.2
  135.6 0.7 constant_dynamic-update-slice_fusion.1
  136.3 3.2 %collective-permute-done.14 = bf16[1024,128]{0,1:T(8,128)(2,1)S(1)} collective-permute-done((bf16[1024,128]{0,1:T(8,128)(2,1)S(1)}, bf16[1024,128]{0,1:T(8,128)(2,1)S(1)}, u32[]{:S(2)}, u32[]{:S(2)}) %collective-permute-start.14) | collective-permute-done | bytes 262176 | tf_op jit(solution)/shard_map/ppermute | solution.py:85
  139.6 0.7 constant_dynamic-update-slice_fusion
  140.3 3.5 %gather_fusion = bf16[64,1024]{1,0:T(8,128)(2,1)S(1)} fusion(bf16[1024,2048]{0,1:T(8,128)(2,1)} %constant_dynamic-update-slice_fusion, s32[1024]{0:T(1024)S(1)} %pad_clamp_fusion.1), kind=kCustom, calls=%fused_computation.clone | custom fusion | bytes 262400 | tf_op jit(solution)/shard_map/jit(_take)/gather | solution.py:98
  143.8 3.5 %gather_fusion.1 = bf16[64,1024]{1,0:T(8,128)(2,1)S(1)} fusion(bf16[1024,2048]{0,1:T(8,128)(2,1)} %constant_dynamic-update-slice_fusion, s32[1024]{0:T(1024)S(1)} %pad_clamp_fusion), kind=kCustom, calls=%fused_computation.1.clone | custom fusion | bytes 262400 | tf_op jit(solution)/shard_map/jit(_take)/gather | solution.py:99
  147.5 16.3 %while.10 = (s32[]{:T(128)}, bf16[2,32,64,256]{3,2,1,0:T(8,128)(2,1)S(1)}, f32[1024,64]{0,1:T(8,128)S(1)}, s32[2]{0:T(128)S(1)}, bf16[1024,64]{0,1:T(8,128)(2,1)...) while((s32[]{:T(128)}, ...), condition=%wide.region_3.5_spmd, body=%wide.region_2.4_spmd.sunk | while | flops 2181103616 | bytes 25297088 | solution.py:115
  150.3 2.8 add_convert_fusion.2
  153.1 2.5 bitcast_dynamic-update-slice_fusion.2
  158.4 2.8 add_convert_fusion.2
  161.2 2.5 bitcast_dynamic-update-slice_fusion.2
  163.8 1.3 copy-done.1
  165.3 36.1 %reduce-scatter.2.cloned.1.call-done = bf16[32,64,256]{2,1,0:T(8,128)(2,1)} async-done(((bf16[64,64,256]{2,1,0:T(8,128)(2,1)}), bf16[32,64,256]{2,1,0:T(8,128)(2,1)}) %reduce-scatter.2.cloned.1.call-update) | async-done | bytes 1048592 | tf_op jit(solution)/shard_map/reduce_scatter | solution.py:116
  201.5 1.6 fusion.18
  203.1 2.3 convert_bitcast_fusion
  205.4 1.8 copy.17
  207.2 76.3 %all_to_all.18 = bf16[192,1,32,256]{3,2,1,0:T(8,128)(2,1)S(1)} all-to-all(bf16[192,1,32,256]{3,2,1,0:T(8,128)(2,1)S(1)} %copy.17), channel_id=1, replica_groups=mesh['run'=1,'row'=16,'col'=1,'seg'=2] {'row'}, dimensions={0} | all-to-all | bytes 6291456 | tf_op jit(solution)/shard_map/all_to_all | solution.py:138
  283.5 2.1 copy.18
  (60 shorter events, 4.8 us)
Async XLA Ops:
  6.5 1.0 copy-start
  6.5 194.9 %reduce-scatter.2.cloned.1.call-start = ((), (), s32[]{:S(2)}) async-start(), calls=%async_computation.2 | async-start | bytes 3145728 | tf_op jit(solution)/shard_map/reduce_scatter | solution.py:116
  38.8 31.9 %copy-start.4 = (s32[64]{0:T(128)S(1)}, s32[64]{0:T(128)}, u32[]{:S(2)}) copy-start(s32[64]{0:T(128)} %param.9) | copy-start | bytes 772
  70.1 12.8 %copy-start.3 = (s32[64]{0:T(128)S(1)}, s32[64]{0:T(128)}, u32[]{:S(2)}) copy-start(s32[64]{0:T(128)} %param.10) | copy-start | bytes 772
  71.2 11.8 %collective-permute-start = (bf16[1024,128]{0,1:T(8,128)(2,1)S(1)}, bf16[1024,128]{0,1:T(8,128)(2,1)S(1)}, u32[]{:S(2)}, u32[]{:S(2)}) collective-permute-start(bf16[1024,128]{0,1:T(8,128)(2,1)S(1)} %bitcast.42), channel_id=1, source_target_pairs={{0,2},{2,4},{4,6},{6,8},{8,10},{10,12},{12,14},{14,16},{16,18},{18... | collective-permute-start | bytes 786440 | tf_op jit(solution)/shard_map/ppermute | solution.py:85
  73.9 10.9 %collective-permute-start.1 = (bf16[1024,128]{0,1:T(8,128)(2,1)S(1)}, bf16[1024,128]{0,1:T(8,128)(2,1)S(1)}, u32[]{:S(2)}, u32[]{:S(2)}) collective-permute-start(bf16[1024,128]{0,1:T(8,128)(2,1)S(1)} %bitcast.43), channel_id=1, source_target_pairs={{0,30},{2,0},{4,2},{6,4},{8,6},{10,8},{12,10},{14,12},{16,14},{18,... | collective-permute-start | bytes 786440 | tf_op jit(solution)/shard_map/ppermute | solution.py:90
  83.0 5.1 %collective-permute-start.2 = (bf16[1024,128]{0,1:T(8,128)(2,1)S(1)}, bf16[1024,128]{0,1:T(8,128)(2,1)S(1)}, u32[]{:S(2)}, u32[]{:S(2)}) collective-permute-start(bf16[1024,128]{0,1:T(8,128)(2,1)S(1)} %collective-permute-done), channel_id=1, source_target_pairs={{0,2},{2,4},{4,6},{6,8},{8,10},{10,12},{12,14},{14,16},{16,18},{18... | collective-permute-start | bytes 786440 | tf_op jit(solution)/shard_map/ppermute | solution.py:85
  84.8 9.0 %collective-permute-start.3 = (bf16[1024,128]{0,1:T(8,128)(2,1)S(1)}, bf16[1024,128]{0,1:T(8,128)(2,1)}, u32[]{:S(2)}, u32[]{:S(2)}) collective-permute-start(bf16[1024,128]{0,1:T(8,128)(2,1)S(1)} %collective-permute-done.1), channel_id=1, source_target_pairs={{0,30},{2,0},{4,2},{6,4},{8,6},{10,8},{12,10},{14,12},{16,14},{18,... | collective-permute-start | bytes 786440 | tf_op jit(solution)/shard_map/ppermute | solution.py:90
  88.1 9.6 %collective-permute-start.4 = (bf16[1024,128]{0,1:T(8,128)(2,1)S(1)}, bf16[1024,128]{0,1:T(8,128)(2,1)}, u32[]{:S(2)}, u32[]{:S(2)}) collective-permute-start(bf16[1024,128]{0,1:T(8,128)(2,1)S(1)} %collective-permute-done.2), channel_id=1, source_target_pairs={{0,2},{2,4},{4,6},{6,8},{8,10},{10,12},{12,14},{14,16},{16,18},{18... | collective-permute-start | bytes 786440 | tf_op jit(solution)/shard_map/ppermute | solution.py:85
  93.8 8.9 %collective-permute-start.5 = (bf16[1024,128]{0,1:T(8,128)(2,1)}, bf16[1024,128]{0,1:T(8,128)(2,1)}, u32[]{:S(2)}, u32[]{:S(2)}) collective-permute-start(bf16[1024,128]{0,1:T(8,128)(2,1)} %collective-permute-done.3), channel_id=1, source_target_pairs={{0,30},{2,0},{4,2},{6,4},{8,6},{10,8},{12,10},{14,12},{16,14},{18,... | collective-permute-start | bytes 786440 | tf_op jit(solution)/shard_map/ppermute | solution.py:90
  97.7 9.3 %collective-permute-start.6 = (bf16[1024,128]{0,1:T(8,128)(2,1)}, bf16[1024,128]{0,1:T(8,128)(2,1)}, u32[]{:S(2)}, u32[]{:S(2)}) collective-permute-start(bf16[1024,128]{0,1:T(8,128)(2,1)} %collective-permute-done.4), channel_id=1, source_target_pairs={{0,2},{2,4},{4,6},{6,8},{8,10},{10,12},{12,14},{14,16},{16,18},{18... | collective-permute-start | bytes 786440 | tf_op jit(solution)/shard_map/ppermute | solution.py:85
  102.7 8.9 %collective-permute-start.7 = (bf16[1024,128]{0,1:T(8,128)(2,1)}, bf16[1024,128]{0,1:T(8,128)(2,1)S(1)}, u32[]{:S(2)}, u32[]{:S(2)}) collective-permute-start(bf16[1024,128]{0,1:T(8,128)(2,1)} %collective-permute-done.5), channel_id=1, source_target_pairs={{0,30},{2,0},{4,2},{6,4},{8,6},{10,8},{12,10},{14,12},{16,14},{18,... | collective-permute-start | bytes 786440 | tf_op jit(solution)/shard_map/ppermute | solution.py:90
  107.1 9.8 %collective-permute-start.8 = (bf16[1024,128]{0,1:T(8,128)(2,1)}, bf16[1024,128]{0,1:T(8,128)(2,1)S(1)}, u32[]{:S(2)}, u32[]{:S(2)}) collective-permute-start(bf16[1024,128]{0,1:T(8,128)(2,1)} %collective-permute-done.6), channel_id=1, source_target_pairs={{0,2},{2,4},{4,6},{6,8},{8,10},{10,12},{12,14},{14,16},{16,18},{18... | collective-permute-start | bytes 786440 | tf_op jit(solution)/shard_map/ppermute | solution.py:85
  111.6 8.6 %collective-permute-start.9 = (bf16[1024,128]{0,1:T(8,128)(2,1)S(1)}, bf16[1024,128]{0,1:T(8,128)(2,1)S(1)}, u32[]{:S(2)}, u32[]{:S(2)}) collective-permute-start(bf16[1024,128]{0,1:T(8,128)(2,1)S(1)} %collective-permute-done.7), channel_id=1, source_target_pairs={{0,30},{2,0},{4,2},{6,4},{8,6},{10,8},{12,10},{14,12},{16,14},{18,... | collective-permute-start | bytes 786440 | tf_op jit(solution)/shard_map/ppermute | solution.py:90
  116.8 8.7 %collective-permute-start.10 = (bf16[1024,128]{0,1:T(8,128)(2,1)S(1)}, bf16[1024,128]{0,1:T(8,128)(2,1)S(1)}, u32[]{:S(2)}, u32[]{:S(2)}) collective-permute-start(bf16[1024,128]{0,1:T(8,128)(2,1)S(1)} %collective-permute-done.8), channel_id=1, source_target_pairs={{0,2},{2,4},{4,6},{6,8},{8,10},{10,12},{12,14},{14,16},{16,18},{18... | collective-permute-start | bytes 786440 | tf_op jit(solution)/shard_map/ppermute | solution.py:85
  120.2 6.8 %collective-permute-start.11 = (bf16[1024,128]{0,1:T(8,128)(2,1)S(1)}, bf16[1024,128]{0,1:T(8,128)(2,1)S(1)}, u32[]{:S(2)}, u32[]{:S(2)}) collective-permute-start(bf16[1024,128]{0,1:T(8,128)(2,1)S(1)} %collective-permute-done.9), channel_id=1, source_target_pairs={{0,30},{2,0},{4,2},{6,4},{8,6},{10,8},{12,10},{14,12},{16,14},{18,... | collective-permute-start | bytes 786440 | tf_op jit(solution)/shard_map/ppermute | solution.py:90
  125.5 8.3 %collective-permute-start.12 = (bf16[1024,128]{0,1:T(8,128)(2,1)S(1)}, bf16[1024,128]{0,1:T(8,128)(2,1)S(1)}, u32[]{:S(2)}, u32[]{:S(2)}) collective-permute-start(bf16[1024,128]{0,1:T(8,128)(2,1)S(1)} %collective-permute-done.10), channel_id=1, source_target_pairs={{0,2},{2,4},{4,6},{6,8},{8,10},{10,12},{12,14},{14,16},{16,18},{18... | collective-permute-start | bytes 786440 | tf_op jit(solution)/shard_map/ppermute | solution.py:85
  127.0 8.6 %collective-permute-start.13 = (bf16[1024,128]{0,1:T(8,128)(2,1)S(1)}, bf16[1024,128]{0,1:T(8,128)(2,1)S(1)}, u32[]{:S(2)}, u32[]{:S(2)}) collective-permute-start(bf16[1024,128]{0,1:T(8,128)(2,1)S(1)} %collective-permute-done.11), channel_id=1, source_target_pairs={{0,30},{2,0},{4,2},{6,4},{8,6},{10,8},{12,10},{14,12},{16,14},{18,... | collective-permute-start | bytes 786440 | tf_op jit(solution)/shard_map/ppermute | solution.py:90
  133.8 5.7 %collective-permute-start.14 = (bf16[1024,128]{0,1:T(8,128)(2,1)S(1)}, bf16[1024,128]{0,1:T(8,128)(2,1)S(1)}, u32[]{:S(2)}, u32[]{:S(2)}) collective-permute-start(bf16[1024,128]{0,1:T(8,128)(2,1)S(1)} %collective-permute-done.12), channel_id=1, source_target_pairs={{0,2},{2,4},{4,6},{6,8},{8,10},{10,12},{12,14},{14,16},{16,18},{18... | collective-permute-start | bytes 786440 | tf_op jit(solution)/shard_map/ppermute | solution.py:85
  147.5 17.7 %copy-start.5 = (s32[64,1]{0,1:T(1,128)S(1)}, s32[64,1]{0,1:T(1,128)}, u32[]{:S(2)}) copy-start(s32[64,1]{0,1:T(1,128)} %param.11) | copy-start | bytes 772
  150.3 2.8 copy-start.2
  158.4 2.8 copy-start.2
  163.8 1.3 copy-start.1
Sparse Core Ops, SparseCore 0:
  165.3 36.1 reduce-scatter.1
